TPU v7x, 256 devices: a whole 4x4x8 slice. The times are simulated.
256 devices in a mesh: section: 16 (over y_hi, z), seq: 16 (over y_lo, x, core).
Axes of the slice: x: 4, y: 4 (y_hi: 2, y_lo: 2; y = y_hi * 2 + y_lo), z: 8, core: 2. Of those that a mesh axis runs over, the one named last changes fastest.
Arguments:
- stream: bfloat16 [16, 2048, 2048], P('section', 'seq'), may hold values from -6 to 6
- queries: bfloat16 [16, 2048, 2048], P('section', 'seq'), may hold values from -5 to 5
- key_rows: bfloat16 [16, 2048, 2048], P('section', 'seq'), may hold values from -5 to 5
- value_rows: bfloat16 [16, 2048, 2048], P('section', 'seq'), may hold values from -6 to 6
- o_weight: bfloat16 [16, 2048, 2048], P('section', 'seq'), may hold values from -0.125 to 0.125
- norm_gain: float32 [16, 2048], P('section'), may hold values from 0.1 to 1.9
- w_gate: bfloat16 [16, 2048, 7168], P('section', None, 'seq'), may hold values from -0.125 to 0.125
- w_up: bfloat16 [16, 2048, 7168], P('section', None, 'seq'), may hold values from -0.125 to 0.125
- w_down: bfloat16 [16, 7168, 2048], P('section', 'seq'), may hold values from -0.0625 to 0.0625
Outputs:
- passed: bfloat16 [16, 2048, 2048], P('section', 'seq')
All inputs are finite; a program needn't handle non-finite values.
Results may differ from a plain program's by a relative error of at most 0.012.
Values may be sent and summed in bfloat16 or wider, within the bound.
No kernel may reach another device: no remote copies, remote signals or barrier semaphores. Data moves between devices by JAX's collectives and lax.ppermute only.
A program may use at most 64 MiB of HBM per device.

v0:
```python
import jax
import jax.numpy as jnp
from jax import lax
from jax.sharding import PartitionSpec as P

HEADS = 16
HEAD_DIM = 128


def passed_along(block, axis, distance):
    devices = range(lax.axis_size(axis))
    route = [((i - distance) % len(devices), i) for i in devices]
    return lax.ppermute(block, axis, route)


def attend(queries, key_rows, value_rows):
    length = queries.shape[0]
    head_count = queries.shape[1]
    head_width = queries.shape[2]
    block = 512
    count = length // block
    query_blocks = queries.reshape(count, block, head_count, head_width)

    def one_block(pieces):
        block_index, query_block = pieces
        scores = jnp.einsum(
            "qhd,khd->hqk", query_block, key_rows, preferred_element_type=jnp.float32
        ) * head_width ** (-0.5)
        row_pos = lax.broadcasted_iota(jnp.int32, (block, length), 0) + block_index * block
        col_pos = lax.broadcasted_iota(jnp.int32, (block, length), 1)
        scores = jnp.where((col_pos <= row_pos)[None], scores, -1e30)
        highest = jnp.max(scores, axis=-1, keepdims=True)
        powers = jnp.exp(scores - highest)
        weights = (powers / jnp.sum(powers, axis=-1, keepdims=True)).astype(jnp.bfloat16)
        mixture = jnp.einsum(
            "hqk,khd->qhd", weights, value_rows, preferred_element_type=jnp.float32
        )
        return mixture.astype(jnp.bfloat16)

    mixed = lax.map(one_block, (jnp.arange(count, dtype=jnp.int32), query_blocks))
    return mixed.reshape(length, head_count, head_width)


def attend_heads(triple):
    length = triple[0].shape[0]
    group = triple[0].shape[2]
    width = triple[0].shape[3]
    flat = [piece.reshape(length, group, width) for piece in triple]
    mixed = attend(flat[0], flat[1], flat[2])
    return mixed.reshape(length, 1, group, width)


def shards(stream, queries, key_rows, value_rows, o_weight, norm_gain, w_gate, w_up, w_down):
    local_steps = stream.shape[1]
    model_width = stream.shape[2]
    groups = lax.axis_size("seq")
    group_heads = HEADS // groups
    block_rows = HEADS * HEAD_DIM // groups

    def split_heads(tensor):
        return tensor[0].reshape(local_steps, groups, group_heads, HEAD_DIM)

    attended = attend_heads(
        (
            lax.all_to_all(split_heads(queries), "seq", split_axis=1, concat_axis=0, tiled=True),
            lax.all_to_all(split_heads(key_rows), "seq", split_axis=1, concat_axis=0, tiled=True),
            lax.all_to_all(split_heads(value_rows), "seq", split_axis=1, concat_axis=0, tiled=True),
        )
    )
    returned = lax.all_to_all(attended, "seq", split_axis=0, concat_axis=1, tiled=True)
    flat_rows = returned.reshape(local_steps, HEADS * HEAD_DIM)
    piece = lax.all_gather(o_weight[0], "seq", axis=0, tiled=True)
    count = piece.shape[0] // block_rows
    columns = flat_rows.reshape(local_steps, count, block_rows)
    shaped = piece.reshape(count, block_rows, model_width)
    parts = jnp.einsum("tkb,kbd->ktd", columns, shaped, preferred_element_type=jnp.float32).astype(
        jnp.bfloat16
    )
    parts = lax.optimization_barrier(parts)
    projected = jnp.sum(parts.astype(jnp.float32), axis=0)
    residual = stream[0].astype(jnp.float32) + projected
    normed = (
        residual
        * lax.rsqrt(jnp.mean(residual * residual, axis=-1, keepdims=True) + 1e-05)
        * norm_gain[0]
    ).astype(jnp.bfloat16)
    gate_local = w_gate[0]
    up_local = w_up[0]
    down_local = w_down[0]
    piece = lax.all_gather(normed, "seq", axis=0, tiled=True)
    gate_pre = jnp.dot(piece, gate_local, preferred_element_type=jnp.float32)
    up_pre = jnp.dot(piece, up_local, preferred_element_type=jnp.float32)
    hidden = (jax.nn.silu(gate_pre) * up_pre).astype(jnp.bfloat16)
    partials = jnp.dot(hidden, down_local, preferred_element_type=jnp.float32)
    ffn_sum = lax.psum_scatter(
        partials.astype(jnp.bfloat16), "seq", scatter_dimension=0, tiled=True
    ).astype(jnp.float32)
    finished = (residual + ffn_sum).astype(jnp.bfloat16)
    passed = passed_along(finished, "section", 1)
    return passed[None]


def solution(mesh):
    placed = (
        P("section", "seq", None),
        P("section", "seq", None),
        P("section", "seq", None),
        P("section", "seq", None),
        P("section", "seq", None),
        P("section", None),
        P("section", None, "seq"),
        P("section", None, "seq"),
        P("section", "seq", None),
    )
    return jax.shard_map(
        shards, mesh=mesh, in_specs=placed, out_specs=P("section", "seq", None), check_vma=False
    )
```

profile of v0, /device:TPU:7, one launch (start us, length us, event | category | flops | bytes accessed | tf_op | source)
XLA Modules:
  0.0 287.4 jit_solution(17072727347162290342)
XLA Ops:
  6.5 0.0 copy-start
  6.5 0.0 all-gather.6.cloned.1.call-start
  6.5 0.7 all-gather.6.cloned.1.call-update
  7.3 2.0 copy.31
  9.3 6.1 %all-to-all-start = ((bf16[128,16,1,128]{0,3,2,1:T(8,128)(2,1)}), bf16[128,16,1,128]{0,3,2,1:T(8,128)(2,1)S(1)}, u32[]{:S(2)}, u32[]{:S(2)}) async-start(bf16[128,16,1,128]{0,3,2,1:T(8,128)(2,1)} %bitcast.10), calls=%async_computation | async-start | bytes 1048576 | tf_op jit(solution)/shard_map/all_to_all | solution.py:65
  15.4 2.1 copy.34
  17.5 6.4 %all-to-all-done = bf16[128,16,1,128]{0,3,2,1:T(8,128)(2,1)S(1)} async-done(((bf16[128,16,1,128]{0,3,2,1:T(8,128)(2,1)}), bf16[128,16,1,128]{0,3,2,1:T(8,128)(2,1)S(1)}, u32[]{:S(2)}, u32[]{:S(2)}) %all-to-all-start) | async-done | bytes 524320 | tf_op jit(solution)/shard_map/all_to_all | solution.py:65
  23.9 5.8 %all-to-all-start.1 = ((bf16[128,16,1,128]{0,3,2,1:T(8,128)(2,1)}), bf16[128,16,1,128]{0,3,2,1:T(8,128)(2,1)S(1)}, u32[]{:S(2)}, u32[]{:S(2)}) async-start(bf16[128,16,1,128]{0,3,2,1:T(8,128)(2,1)} %bitcast.16), calls=%async_computation.1 | async-start | bytes 1048576 | tf_op jit(solution)/shard_map/all_to_all | solution.py:66
  29.7 0.0 copy-done.2
  29.7 1.0 copy.37
  30.8 12.6 %all-to-all-done.1 = bf16[128,16,1,128]{0,3,2,1:T(8,128)(2,1)S(1)} async-done(((bf16[128,16,1,128]{0,3,2,1:T(8,128)(2,1)}), bf16[128,16,1,128]{0,3,2,1:T(8,128)(2,1)S(1)}, u32[]{:S(2)}, u32[]{:S(2)}) %all-to-all-start.1) | async-done | bytes 524320 | tf_op jit(solution)/shard_map/all_to_all | solution.py:66
  43.4 5.9 %all-to-all-start.2 = ((bf16[128,16,1,128]{0,3,2,1:T(8,128)(2,1)}), bf16[128,16,1,128]{0,3,2,1:T(8,128)(2,1)S(1)}, u32[]{:S(2)}, u32[]{:S(2)}) async-start(bf16[128,16,1,128]{0,3,2,1:T(8,128)(2,1)} %bitcast.21), calls=%async_computation.2 | async-start | bytes 1048576 | tf_op jit(solution)/shard_map/all_to_all | solution.py:67
  49.3 0.0 all-gather.4.cloned.1.call-start
  49.4 1.1 copy.33
  50.4 0.3 copy.36
  50.7 12.2 %all-to-all-done.2 = bf16[128,16,1,128]{0,3,2,1:T(8,128)(2,1)S(1)} async-done(((bf16[128,16,1,128]{0,3,2,1:T(8,128)(2,1)}), bf16[128,16,1,128]{0,3,2,1:T(8,128)(2,1)S(1)}, u32[]{:S(2)}, u32[]{:S(2)}) %all-to-all-start.2) | async-done | bytes 524320 | tf_op jit(solution)/shard_map/all_to_all | solution.py:67
  62.9 0.3 copy.39
  63.2 21.5 %while.10 = (s32[]{:T(128)}, bf16[4,512,1,128]{3,1,2,0:T(8,128)(2,1)}, s32[4]{0:T(128)S(1)}, bf16[4,512,1,128]{3,1,2,0:T(8,128)(2,1)}, bf16[2048,1,128]{2,0,1:T(...) while((s32[]{:T(128)}, bf16[4,512,1,128]{3,1,2,0:T(8,128)(2,1)}, ...), condition=%wide.region_3.4_spmd, body=%wide.region_0.3_spmd.sunk | while | flops 546373120 | bytes 13908097 | solution.py:40
  63.2 0.6 dynamic_slice.17
  64.5 1.9 fusion.25
  66.4 0.7 fusion.26
  67.1 1.5 fusion.27
  68.6 0.6 dynamic_slice.17
  69.9 1.9 fusion.25
  71.7 0.7 fusion.26
  72.5 1.5 fusion.27
  74.0 0.6 dynamic_slice.17
  75.2 1.9 fusion.25
  77.1 0.7 fusion.26
  77.8 1.5 fusion.27
  79.4 0.6 dynamic_slice.17
  80.6 1.9 fusion.25
  82.5 0.7 fusion.26
  83.2 1.5 fusion.27
  84.7 0.5 broadcast.27
  85.3 2.0 reduce.4
  87.3 0.1 reshape.62
  87.5 14.2 %all_to_all.60 = bf16[16,2,8192]{2,1,0:T(2,128)(2,1)S(1)} all-to-all(bf16[16,2,8192]{2,1,0:T(2,128)(2,1)S(1)} %reshape.62), channel_id=1, replica_groups=mesh['section'=16,'seq'=16] {'seq'}, dimensions={0} | all-to-all | bytes 1048576 | tf_op jit(solution)/shard_map/all_to_all | solution.py:70
  101.7 0.5 reshape.63
  102.2 0.1 copy.42
  102.3 0.0 all-gather.6.cloned.1.call-done
  102.3 5.7 %convolution_convert_fusion.1 = bf16[16,128,2048]{2,1,0:T(8,128)(2,1)S(1)} fusion(bf16[128,16,128]{2,0,1:T(8,128)(2,1)S(1)} %bitcast.93, bf16[16,128,2048]{2,1,0:T(8,128)(2,1)} %bitcast.92), kind=kOutput, calls=%fused_computation.17 | convolution fusion | flops 1077936128 | bytes 17301504 | tf_op jit(solution)/shard_map/tkb,kbd->ktd/dot_general | solution.py:76
  108.0 0.0 copy-start.1
  108.1 0.0 copy-start.3
  108.1 1.8 convert_reduce_fusion
  109.9 0.0 copy-done.1
  109.9 0.2 multiply_reduce_fusion
  110.2 0.0 copy-done.3
  110.2 1.0 multiply_convert_fusion.1
  111.1 0.0 all-gather.4.cloned.1.call-update
  111.2 0.2 reduce-scatter.2.cloned.1.call-start
  111.4 56.7 %all-gather.4.cloned.1.call-done = bf16[2048,2048]{1,0:T(8,128)(2,1)} async-done(((bf16[128,2048]{1,0:T(8,128)(2,1)}), bf16[2048,2048]{1,0:T(8,128)(2,1)}) %all-gather.4.cloned.1.call-update) | async-done | bytes 8388624 | tf_op jit(solution)/shard_map/all_gather | solution.py:90
  168.1 7.2 %fusion.12 = f32[2048,448]{0,1:T(8,128)S(1)} fusion(bf16[2048,2048]{1,0:T(8,128)(2,1)} %all-gather.4.cloned.1.call-done, bf16[1,2048,448]{1,2,0:T(8,128)(2,1)} %param.17), kind=kOutput, calls=%fused_computation.21 | convolution fusion | flops 3758096384 | bytes 13893632 | tf_op jit(solution)/shard_map/dot_general | solution.py:91
  175.3 0.0 copy-done.4
  175.3 0.0 copy-done.5
  175.3 4.3 %multiply_convert_fusion = bf16[2048,448]{0,1:T(8,128)(2,1)S(1)} fusion(f32[2048,448]{0,1:T(8,128)S(1)} %fusion.12, bf16[2048,2048]{1,0:T(8,128)(2,1)S(1)} %copy-done.4, bf16[1,2048,448]{1,2,0:T(8,128)(2,1)S(1)} %copy-done.5), kind=kOutput, calls=%fused_computation.18 | convolution fusion | flops 3763601408 | bytes 15728640 | tf_op jit(solution)/shard_map/dot_general | solution.py:92
  179.6 0.0 copy-done
  179.6 6.9 %convolution_convert_fusion = bf16[2048,2048]{1,0:T(8,128)(2,1)} fusion(bf16[2048,448]{0,1:T(8,128)(2,1)S(1)} %multiply_convert_fusion, bf16[1,448,2048]{2,1,0:T(8,128)(2,1)S(1)} %copy-done), kind=kOutput, calls=%fused_computation.16 | convolution fusion | flops 3762290688 | bytes 12058624 | tf_op jit(solution)/shard_map/dot_general | solution.py:94
  186.5 0.0 reduce-scatter.2.cloned.1.call-update
  186.5 76.5 %reduce-scatter.2.cloned.1.call-done = bf16[128,2048]{1,0:T(8,128)(2,1)} async-done(((bf16[2048,2048]{1,0:T(8,128)(2,1)}), bf16[128,2048]{1,0:T(8,128)(2,1)}) %reduce-scatter.2.cloned.1.call-update) | async-done | bytes 524304 | tf_op jit(solution)/shard_map/reduce_scatter | solution.py:95
  263.0 1.2 add_convert_fusion
  264.3 1.3 collective-permute-start
  265.6 14.5 %collective-permute-done = bf16[128,2048]{1,0:T(8,128)(2,1)S(1)} collective-permute-done((bf16[128,2048]{1,0:T(8,128)(2,1)S(1)}, bf16[128,2048]{1,0:T(8,128)(2,1)S(1)}, u32[]{:S(2)}, u32[]{:S(2)}) %collective-permute-start) | collective-permute-done | bytes 524320 | tf_op jit(solution)/shard_map/ppermute | solution.py:13
  280.1 0.8 copy.54
  (10 shorter events, 0.0 us)
Async XLA Ops:
  6.5 173.1 %copy-start = (bf16[1,448,2048]{2,1,0:T(8,128)(2,1)S(1)}, bf16[1,448,2048]{2,1,0:T(8,128)(2,1)}, u32[]{:S(2)}) copy-start(bf16[1,448,2048]{2,1,0:T(8,128)(2,1)} %param.19) | copy-start | bytes 5505028
  6.5 23.2 %copy-start.2 = (bf16[1,128,2048]{2,1,0:T(8,128)(2,1)S(1)}, bf16[1,128,2048]{2,1,0:T(8,128)(2,1)}, u32[]{:S(2)}) copy-start(bf16[1,128,2048]{2,1,0:T(8,128)(2,1)} %param.14) | copy-start | bytes 1572868
  6.5 95.8 %all-gather.6.cloned.1.call-start = ((), (), s32[]{:S(2)}) async-start(), calls=%async_computation.7 | async-start | bytes 8912896 | tf_op jit(solution)/shard_map/all_gather | solution.py:72
  9.3 14.6 %all-to-all-start = ((bf16[128,16,1,128]{0,3,2,1:T(8,128)(2,1)}), bf16[128,16,1,128]{0,3,2,1:T(8,128)(2,1)S(1)}, u32[]{:S(2)}, u32[]{:S(2)}) async-start(bf16[128,16,1,128]{0,3,2,1:T(8,128)(2,1)} %bitcast.10), calls=%async_computation | async-start | bytes 1048576 | tf_op jit(solution)/shard_map/all_to_all | solution.py:65
  23.9 19.5 %all-to-all-start.1 = ((bf16[128,16,1,128]{0,3,2,1:T(8,128)(2,1)}), bf16[128,16,1,128]{0,3,2,1:T(8,128)(2,1)S(1)}, u32[]{:S(2)}, u32[]{:S(2)}) async-start(bf16[128,16,1,128]{0,3,2,1:T(8,128)(2,1)} %bitcast.16), calls=%async_computation.1 | async-start | bytes 1048576 | tf_op jit(solution)/shard_map/all_to_all | solution.py:66
  43.4 19.6 %all-to-all-start.2 = ((bf16[128,16,1,128]{0,3,2,1:T(8,128)(2,1)}), bf16[128,16,1,128]{0,3,2,1:T(8,128)(2,1)S(1)}, u32[]{:S(2)}, u32[]{:S(2)}) async-start(bf16[128,16,1,128]{0,3,2,1:T(8,128)(2,1)} %bitcast.21), calls=%async_computation.2 | async-start | bytes 1048576 | tf_op jit(solution)/shard_map/all_to_all | solution.py:67
  49.3 118.8 %all-gather.4.cloned.1.call-start = ((), (), s32[]{:S(2)}) async-start(), calls=%async_computation.5 | async-start | bytes 8912896 | tf_op jit(solution)/shard_map/all_gather | solution.py:90
  108.0 1.9 copy-start.1
  108.1 2.1 copy-start.3
  111.2 151.9 %reduce-scatter.2.cloned.1.call-start = ((), (), s32[]{:S(2)}) async-start(), calls=%async_computation.6 | async-start | bytes 8912896 | tf_op jit(solution)/shard_map/reduce_scatter | solution.py:95
  168.1 7.2 %copy-start.4 = (bf16[2048,2048]{1,0:T(8,128)(2,1)S(1)}, bf16[2048,2048]{1,0:T(8,128)(2,1)}, u32[]{:S(2)}) copy-start(bf16[2048,2048]{1,0:T(8,128)(2,1)} %all-gather.4.cloned.1.call-done) | copy-start | bytes 25165828
  168.1 7.2 %copy-start.5 = (bf16[1,2048,448]{1,2,0:T(8,128)(2,1)S(1)}, bf16[1,2048,448]{1,2,0:T(8,128)(2,1)}, u32[]{:S(2)}) copy-start(bf16[1,2048,448]{1,2,0:T(8,128)(2,1)} %param.18) | copy-start | bytes 5505028
  264.3 15.8 %collective-permute-start = (bf16[128,2048]{1,0:T(8,128)(2,1)S(1)}, bf16[128,2048]{1,0:T(8,128)(2,1)S(1)}, u32[]{:S(2)}, u32[]{:S(2)}) collective-permute-start(bf16[128,2048]{1,0:T(8,128)(2,1)S(1)} %add_convert_fusion), channel_id=1, source_target_pairs={{240,0},{0,16},{16,32},{32,48},{48,64},{64,80},{80,96},{96,112},{1... | collective-permute-start | bytes 1572872 | tf_op jit(solution)/shard_map/ppermute | solution.py:13
Sparse Core Ops, SparseCore 0:
  9.2 69.0 all-gather.5
  111.3 56.7 all-gather.3
  186.6 76.3 reduce-scatter.1
where the time goes:
time: 288 us; the launch traced here: 287 us
  waiting for transfers between devices  180 us (62%)
  matrix products  37.7 us (13%)
  starting transfers between devices  19.4 us (7%)
  blocking collectives  14.2 us (5%)
  between operations  13.3 us (5%)
  local copies, waits for them, and re-layouts  11.3 us (4%)
  other arithmetic  9.18 us (3%)
    reduce_scatter x1, waiting for transfers between devices, shards(): lax.psum_scatter(partials.astype(jnp.bfloat16), 'seq', scatter_dimension=...  76.5 us
    all_gather x1, waiting for transfers between devices, shards(): piece = lax.all_gather(normed, 'seq', axis=0, tiled=True)  56.7 us
    ppermute x1, waiting for transfers between devices, passed_along(): return lax.ppermute(block, axis, route)  14.5 us
    all_to_all x1, blocking collectives, shards(): lax.all_to_all(attended, 'seq', split_axis=0, concat_axis=1, tiled=True)  14.2 us
    all_to_all x1, waiting for transfers between devices, shards(): lax.all_to_all(split_heads(key_rows), 'seq', split_axis=1, concat_axis=0,...  12.6 us
    all_to_all x1, waiting for transfers between devices, shards(): lax.all_to_all(split_heads(value_rows), 'seq', split_axis=1, concat_axis=...  12.2 us
    dot_general x4, matrix products, one_block(): jnp.einsum('qhd,khd->hqk', query_block, key_rows, preferred_element_type=...  7.47 us
    dot_general x1, matrix products, shards(): gate_pre = jnp.dot(piece, gate_local, preferred_element_type=jnp.float32)  7.2 us
  transfers between devices with their start and end apart: 7, of which 6 were waited for; matrix products, arithmetic and copies ran while one was open for 10% of the time, Pallas kernels for 0%

commit v1 on v0

--- a/solution.py
+++ b/solution.py
@@ -87,7 +87,10 @@
     gate_local = w_gate[0]
     up_local = w_up[0]
     down_local = w_down[0]
-    piece = lax.all_gather(normed, "seq", axis=0, tiled=True)
+    screen_spread = lambda join_dim, original, ax_name: jnp.concatenate(
+        lax.all_to_all(jnp.stack(lax.axis_size(ax_name) * [original]), ax_name, 0, 0), axis=join_dim
+    )
+    piece = screen_spread(0, normed, "seq")
     gate_pre = jnp.dot(piece, gate_local, preferred_element_type=jnp.float32)
     up_pre = jnp.dot(piece, up_local, preferred_element_type=jnp.float32)
     hidden = (jax.nn.silu(gate_pre) * up_pre).astype(jnp.bfloat16)

time: 288 us -> 328 us (1.14)
  blocking collectives: 14.2 us -> 112 us
  waiting for transfers between devices: 180 us -> 124 us
    all_to_all x0 -> x1, blocking collectives: none -> 97.9 us  [shards(): lax.all_to_all(jnp.stack(lax.axis_size(ax_name) * [original]), ax_name, 0...]
    all_gather x1 -> x0, waiting for transfers between devices: 56.7 us -> none  [shards(): piece = lax.all_gather(normed, 'seq', axis=0, tiled=True)]
  transfers between devices with their start and end apart: 7 -> 6, of which waited for: 6 -> 5; matrix products, arithmetic and copies ran while one was open for 10% -> 9% of each run, Pallas kernels for 0% -> 0%
where the time goes in v1:
time: 328 us; the launch traced here: 327 us
  waiting for transfers between devices  124 us (38%)
  blocking collectives  112 us (34%)
  matrix products  34.6 us (11%)
  starting transfers between devices  19.2 us (6%)
  between operations  13.6 us (4%)
  local copies, waits for them, and re-layouts  12.3 us (4%)
  other arithmetic  8.31 us (3%)
    all_to_all x1, blocking collectives, shards(): lax.all_to_all(jnp.stack(lax.axis_size(ax_name) * [original]), ax_name, 0...  97.9 us
    reduce_scatter x1, waiting for transfers between devices, shards(): lax.psum_scatter(partials.astype(jnp.bfloat16), 'seq', scatter_dimension=...  77.8 us
    ppermute x1, waiting for transfers between devices, passed_along(): return lax.ppermute(block, axis, route)  14.5 us
    all_to_all x1, blocking collectives, shards(): lax.all_to_all(attended, 'seq', split_axis=0, concat_axis=1, tiled=True)  14.2 us
    all_to_all x1, waiting for transfers between devices, shards(): lax.all_to_all(split_heads(key_rows), 'seq', split_axis=1, concat_axis=0,...  12.6 us
    all_to_all x1, waiting for transfers between devices, shards(): lax.all_to_all(split_heads(value_rows), 'seq', split_axis=1, concat_axis=...  12.2 us
    dot_general x4, matrix products, one_block(): jnp.einsum('qhd,khd->hqk', query_block, key_rows, preferred_element_type=...  7.47 us
    dot_general x1, matrix products, shards(): partials = jnp.dot(hidden, down_local, preferred_element_type=jnp.float32)  6.92 us
  transfers between devices with their start and end apart: 6, of which 5 were waited for; matrix products, arithmetic and copies ran while one was open for 9% of the time, Pallas kernels for 0%

profile of v1, /device:TPU:7, one launch (start us, length us, event | category | flops | bytes accessed | tf_op | source)
XLA Modules:
  0.0 327.0 jit_solution(15948059061593022320)
XLA Ops:
  6.5 0.0 copy-start
  6.5 0.0 all-gather.3.cloned.1.call-start
  6.5 0.7 all-gather.3.cloned.1.call-update
  7.3 2.0 copy.31
  9.3 6.1 %all-to-all-start = ((bf16[128,16,1,128]{0,3,2,1:T(8,128)(2,1)}), bf16[128,16,1,128]{0,3,2,1:T(8,128)(2,1)S(1)}, u32[]{:S(2)}, u32[]{:S(2)}) async-start(bf16[128,16,1,128]{0,3,2,1:T(8,128)(2,1)} %bitcast.10), calls=%async_computation | async-start | bytes 1048576 | tf_op jit(solution)/shard_map/all_to_all | solution.py:65
  15.4 2.1 copy.34
  17.5 6.4 %all-to-all-done = bf16[128,16,1,128]{0,3,2,1:T(8,128)(2,1)S(1)} async-done(((bf16[128,16,1,128]{0,3,2,1:T(8,128)(2,1)}), bf16[128,16,1,128]{0,3,2,1:T(8,128)(2,1)S(1)}, u32[]{:S(2)}, u32[]{:S(2)}) %all-to-all-start) | async-done | bytes 524320 | tf_op jit(solution)/shard_map/all_to_all | solution.py:65
  23.9 5.8 %all-to-all-start.1 = ((bf16[128,16,1,128]{0,3,2,1:T(8,128)(2,1)}), bf16[128,16,1,128]{0,3,2,1:T(8,128)(2,1)S(1)}, u32[]{:S(2)}, u32[]{:S(2)}) async-start(bf16[128,16,1,128]{0,3,2,1:T(8,128)(2,1)} %bitcast.16), calls=%async_computation.1 | async-start | bytes 1048576 | tf_op jit(solution)/shard_map/all_to_all | solution.py:66
  29.7 0.0 copy-done.2
  29.7 1.1 copy.37
  30.8 12.6 %all-to-all-done.1 = bf16[128,16,1,128]{0,3,2,1:T(8,128)(2,1)S(1)} async-done(((bf16[128,16,1,128]{0,3,2,1:T(8,128)(2,1)}), bf16[128,16,1,128]{0,3,2,1:T(8,128)(2,1)S(1)}, u32[]{:S(2)}, u32[]{:S(2)}) %all-to-all-start.1) | async-done | bytes 524320 | tf_op jit(solution)/shard_map/all_to_all | solution.py:66
  43.4 5.9 %all-to-all-start.2 = ((bf16[128,16,1,128]{0,3,2,1:T(8,128)(2,1)}), bf16[128,16,1,128]{0,3,2,1:T(8,128)(2,1)S(1)}, u32[]{:S(2)}, u32[]{:S(2)}) async-start(bf16[128,16,1,128]{0,3,2,1:T(8,128)(2,1)} %bitcast.21), calls=%async_computation.2 | async-start | bytes 1048576 | tf_op jit(solution)/shard_map/all_to_all | solution.py:67
  49.3 0.0 reduce-scatter.2.cloned.1.call-start
  49.4 1.0 copy.33
  50.4 0.3 copy.36
  50.7 12.2 %all-to-all-done.2 = bf16[128,16,1,128]{0,3,2,1:T(8,128)(2,1)S(1)} async-done(((bf16[128,16,1,128]{0,3,2,1:T(8,128)(2,1)}), bf16[128,16,1,128]{0,3,2,1:T(8,128)(2,1)S(1)}, u32[]{:S(2)}, u32[]{:S(2)}) %all-to-all-start.2) | async-done | bytes 524320 | tf_op jit(solution)/shard_map/all_to_all | solution.py:67
  62.9 0.3 copy.39
  63.2 21.5 %while.10 = (s32[]{:T(128)}, bf16[4,512,1,128]{3,1,2,0:T(8,128)(2,1)}, s32[4]{0:T(128)S(1)}, bf16[4,512,1,128]{3,1,2,0:T(8,128)(2,1)}, bf16[2048,1,128]{2,0,1:T(...) while((s32[]{:T(128)}, bf16[4,512,1,128]{3,1,2,0:T(8,128)(2,1)}, ...), condition=%wide.region_3.4_spmd, body=%wide.region_0.3_spmd.sunk | while | flops 546373120 | bytes 13908097 | solution.py:40
  63.2 0.6 dynamic_slice.17
  64.5 1.9 fusion.30
  66.4 0.7 fusion.31
  67.1 1.5 fusion.32
  68.6 0.6 dynamic_slice.17
  69.9 1.9 fusion.30
  71.7 0.7 fusion.31
  72.5 1.5 fusion.32
  74.0 0.6 dynamic_slice.17
  75.2 1.9 fusion.30
  77.1 0.7 fusion.31
  77.8 1.5 fusion.32
  79.4 0.6 dynamic_slice.17
  80.6 1.9 fusion.30
  82.5 0.7 fusion.31
  83.2 1.5 fusion.32
  84.7 0.5 broadcast.35
  85.2 2.0 reduce.4
  87.2 0.1 reshape.81
  87.3 14.2 %all_to_all.65 = bf16[16,2,8192]{2,1,0:T(2,128)(2,1)S(1)} all-to-all(bf16[16,2,8192]{2,1,0:T(2,128)(2,1)S(1)} %reshape.81), channel_id=1, replica_groups=mesh['section'=16,'seq'=16] {'seq'}, dimensions={0} | all-to-all | bytes 1048576 | tf_op jit(solution)/shard_map/all_to_all | solution.py:70
  101.5 0.5 reshape.82
  102.1 0.1 copy.42
  102.1 0.0 all-gather.3.cloned.1.call-done
  102.2 5.7 %convolution_convert_fusion.1 = bf16[16,128,2048]{2,1,0:T(8,128)(2,1)S(1)} fusion(bf16[128,16,128]{2,0,1:T(8,128)(2,1)S(1)} %bitcast.101, bf16[16,128,2048]{2,1,0:T(8,128)(2,1)} %bitcast.98), kind=kOutput, calls=%fused_computation.17 | convolution fusion | flops 1077936128 | bytes 17301504 | tf_op jit(solution)/shard_map/tkb,kbd->ktd/dot_general | solution.py:76
  107.9 0.0 copy-start.1
  107.9 0.0 copy-start.3
  107.9 1.8 convert_reduce_fusion
  109.8 0.0 copy-done.1
  109.8 0.2 multiply_reduce_fusion
  110.0 0.0 copy-done.3
  110.0 0.2 fusion.18
  110.2 1.1 stack.5
  111.3 0.0 copy-start.4
  111.3 97.9 %all_to_all.66 = bf16[16,128,2048]{2,1,0:T(8,128)(2,1)S(1)} all-to-all(bf16[16,128,2048]{2,1,0:T(8,128)(2,1)S(1)} %stack.5), channel_id=1, replica_groups=mesh['section'=16,'seq'=16] {'seq'}, dimensions={0} | all-to-all | bytes 16777216 | tf_op jit(solution)/shard_map/all_to_all | solution.py:91
  209.2 0.0 copy-done.4
  209.2 4.0 %fusion.12 = f32[2048,448]{0,1:T(8,128)S(1)} fusion(bf16[2048,2048]{1,0:T(8,128)(2,1)S(1)} %bitcast.99, bf16[1,2048,448]{1,2,0:T(8,128)(2,1)S(1)} %copy-done.4), kind=kOutput, calls=%fused_computation.21 | convolution fusion | flops 3758096384 | bytes 13893632 | tf_op jit(solution)/shard_map/dot_general | solution.py:94
  213.2 0.0 copy-done.5
  213.2 4.3 %multiply_convert_fusion = bf16[2048,448]{0,1:T(8,128)(2,1)S(1)} fusion(f32[2048,448]{0,1:T(8,128)S(1)} %fusion.12, bf16[2048,2048]{1,0:T(8,128)(2,1)S(1)} %bitcast.100, bf16[1,2048,448]{1,2,0:T(8,128)(2,1)S(1)} %copy-done.5), kind=kOutput, calls=%fused_computation.18 | convolution fusion | flops 3763601408 | bytes 15728640 | tf_op jit(solution)/shard_map/dot_general | solution.py:95
  217.5 0.0 copy-done
  217.5 6.9 %convolution_convert_fusion = bf16[2048,2048]{1,0:T(8,128)(2,1)} fusion(bf16[2048,448]{0,1:T(8,128)(2,1)S(1)} %multiply_convert_fusion, bf16[1,448,2048]{2,1,0:T(8,128)(2,1)S(1)} %copy-done), kind=kOutput, calls=%fused_computation.16 | convolution fusion | flops 3762290688 | bytes 12058624 | tf_op jit(solution)/shard_map/dot_general | solution.py:97
  224.5 0.0 reduce-scatter.2.cloned.1.call-update
  224.5 77.8 %reduce-scatter.2.cloned.1.call-done = bf16[128,2048]{1,0:T(8,128)(2,1)} async-done(((bf16[2048,2048]{1,0:T(8,128)(2,1)}), bf16[128,2048]{1,0:T(8,128)(2,1)}) %reduce-scatter.2.cloned.1.call-update) | async-done | bytes 524304 | tf_op jit(solution)/shard_map/reduce_scatter | solution.py:98
  302.3 1.2 add_convert_fusion
  303.5 1.4 collective-permute-start
  304.9 14.5 %collective-permute-done = bf16[128,2048]{1,0:T(8,128)(2,1)S(1)} collective-permute-done((bf16[128,2048]{1,0:T(8,128)(2,1)S(1)}, bf16[128,2048]{1,0:T(8,128)(2,1)S(1)}, u32[]{:S(2)}, u32[]{:S(2)}) %collective-permute-start) | collective-permute-done | bytes 524320 | tf_op jit(solution)/shard_map/ppermute | solution.py:13
  319.3 0.8 copy.54
  (9 shorter events, 0.0 us)
Async XLA Ops:
  6.5 211.0 %copy-start = (bf16[1,448,2048]{2,1,0:T(8,128)(2,1)S(1)}, bf16[1,448,2048]{2,1,0:T(8,128)(2,1)}, u32[]{:S(2)}) copy-start(bf16[1,448,2048]{2,1,0:T(8,128)(2,1)} %param.19) | copy-start | bytes 5505028
  6.5 23.2 %copy-start.2 = (bf16[1,128,2048]{2,1,0:T(8,128)(2,1)S(1)}, bf16[1,128,2048]{2,1,0:T(8,128)(2,1)}, u32[]{:S(2)}) copy-start(bf16[1,128,2048]{2,1,0:T(8,128)(2,1)} %param.14) | copy-start | bytes 1572868
  6.5 95.6 %all-gather.3.cloned.1.call-start = ((), (), s32[]{:S(2)}) async-start(), calls=%async_computation.7 | async-start | bytes 8912896 | tf_op jit(solution)/shard_map/all_gather | solution.py:72
  9.3 14.6 %all-to-all-start = ((bf16[128,16,1,128]{0,3,2,1:T(8,128)(2,1)}), bf16[128,16,1,128]{0,3,2,1:T(8,128)(2,1)S(1)}, u32[]{:S(2)}, u32[]{:S(2)}) async-start(bf16[128,16,1,128]{0,3,2,1:T(8,128)(2,1)} %bitcast.10), calls=%async_computation | async-start | bytes 1048576 | tf_op jit(solution)/shard_map/all_to_all | solution.py:65
  23.9 19.5 %all-to-all-start.1 = ((bf16[128,16,1,128]{0,3,2,1:T(8,128)(2,1)}), bf16[128,16,1,128]{0,3,2,1:T(8,128)(2,1)S(1)}, u32[]{:S(2)}, u32[]{:S(2)}) async-start(bf16[128,16,1,128]{0,3,2,1:T(8,128)(2,1)} %bitcast.16), calls=%async_computation.1 | async-start | bytes 1048576 | tf_op jit(solution)/shard_map/all_to_all | solution.py:66
  43.4 19.6 %all-to-all-start.2 = ((bf16[128,16,1,128]{0,3,2,1:T(8,128)(2,1)}), bf16[128,16,1,128]{0,3,2,1:T(8,128)(2,1)S(1)}, u32[]{:S(2)}, u32[]{:S(2)}) async-start(bf16[128,16,1,128]{0,3,2,1:T(8,128)(2,1)} %bitcast.21), calls=%async_computation.2 | async-start | bytes 1048576 | tf_op jit(solution)/shard_map/all_to_all | solution.py:67
  49.3 253.0 %reduce-scatter.2.cloned.1.call-start = ((), (), s32[]{:S(2)}) async-start(), calls=%async_computation.6 | async-start | bytes 8912896 | tf_op jit(solution)/shard_map/reduce_scatter | solution.py:98
  107.9 1.9 copy-start.1
  107.9 2.1 copy-start.3
  111.3 97.9 %copy-start.4 = (bf16[1,2048,448]{1,2,0:T(8,128)(2,1)S(1)}, bf16[1,2048,448]{1,2,0:T(8,128)(2,1)}, u32[]{:S(2)}) copy-start(bf16[1,2048,448]{1,2,0:T(8,128)(2,1)} %param.17) | copy-start | bytes 5505028
  209.2 4.0 %copy-start.5 = (bf16[1,2048,448]{1,2,0:T(8,128)(2,1)S(1)}, bf16[1,2048,448]{1,2,0:T(8,128)(2,1)}, u32[]{:S(2)}) copy-start(bf16[1,2048,448]{1,2,0:T(8,128)(2,1)} %param.18) | copy-start | bytes 5505028
  303.5 15.8 %collective-permute-start = (bf16[128,2048]{1,0:T(8,128)(2,1)S(1)}, bf16[128,2048]{1,0:T(8,128)(2,1)S(1)}, u32[]{:S(2)}, u32[]{:S(2)}) collective-permute-start(bf16[128,2048]{1,0:T(8,128)(2,1)S(1)} %add_convert_fusion), channel_id=1, source_target_pairs={{240,0},{0,16},{16,32},{32,48},{48,64},{64,80},{80,96},{96,112},{1... | collective-permute-start | bytes 1572872 | tf_op jit(solution)/shard_map/ppermute | solution.py:13
Sparse Core Ops, SparseCore 0:
  9.2 69.0 all-gather.2
  224.6 77.6 reduce-scatter.1
